TPU v7x, 32 devices: a whole 2x2x4 slice. The times are simulated.
32 devices in a mesh: group: 2 (over core), dp: 4 (over z), section: 2 (over x), tensor: 2 (over y).
Axes of the slice: x: 2, y: 2, z: 4, core: 2. Of those that a mesh axis runs over, the one named last changes fastest.
Arguments:
- merged: bfloat16 [768, 5120], P('dp'), may hold values from -6 to 6
- counts: int32 [8], P('dp'), may hold values from 4 to 384
- owners: int32 [768, 1], P('dp'), may hold values from 0 to 3; in each aligned block of 192 rows (0 to 191, 192 to 383, ...) at most 96 rows name the same one
- w_merge: bfloat16 [5120, 8192], P(None, ('group', 'section', 'tensor')), may hold values from -0.078125 to 0.078125
- norm_gain: float32 [8192], P(('group', 'section', 'tensor')), may hold values from 0.25 to 1.75
- cotangent: bfloat16 [4, 4, 96, 8192], P('dp', None, None, ('group', 'section', 'tensor')), may hold values from -6 to 6
Outputs:
- embedded: bfloat16 [4, 4, 96, 8192], P('dp', None, None, ('group', 'section', 'tensor'))
- grad_merged: float32 [768, 5120], P('dp', ('group', 'section', 'tensor'))
- grad_weight: float32 [5120, 8192], P('dp', ('group', 'section', 'tensor'))
Inputs may be any that keep to these rules, and one draw needn't show every extreme that they name: `owners`: in each replica's 192 rows no owner appears more than 96 times.
All inputs are finite; a program needn't handle non-finite values.
Results may differ from a plain program's by a relative error of at most 0.0049.
Values may be sent and summed in bfloat16 or wider, within the bound.
A program may use at most 64 MiB of HBM per device.

v0:
```python
import jax
import jax.numpy as jnp
from jax import lax
from jax.sharding import PartitionSpec as P

D = 8192


def on_device(merged, counts, owners, w_merge, norm_gain, cotangent):
    rows = merged.shape[0]
    columns = w_merge.shape[1]
    replicas = lax.axis_size("dp")
    slots = cotangent.shape[2]
    images = counts.shape[0]
    per_image = rows // images
    projected = jnp.dot(merged, w_merge, preferred_element_type=jnp.float32).astype(jnp.bfloat16)
    row_index = jnp.arange(rows, dtype=jnp.int32)
    image_of = row_index // per_image
    picked = image_of[:, None] == jnp.arange(images, dtype=jnp.int32)[None, :]
    count_of = jnp.sum(jnp.where(picked, counts[None, :], 0), axis=1)
    valid = (4 * (row_index % per_image) < count_of).astype(jnp.float32)
    masked = (projected.astype(jnp.float32) * valid[:, None]).astype(jnp.bfloat16)
    owner = owners[:, 0]
    hits = (owner[:, None] == jnp.arange(replicas, dtype=jnp.int32)[None, :]).astype(jnp.int32)
    before = jnp.cumsum(hits, axis=0) - hits
    slot_index = jnp.sum(before * hits, axis=1)
    target = owner * slots + slot_index
    placer = (jnp.arange(replicas * slots, dtype=jnp.int32)[:, None] == target[None, :]).astype(
        jnp.bfloat16
    )
    outgoing = jnp.dot(placer, masked, preferred_element_type=jnp.float32).astype(jnp.bfloat16)
    outgoing = outgoing.reshape(replicas, slots, columns)
    received = lax.all_to_all(outgoing, "dp", split_axis=0, concat_axis=0, tiled=True)
    values = received.astype(jnp.float32)
    square_sums = lax.psum(jnp.sum(values * values, axis=2), ("group", "section", "tensor"))
    scale = lax.rsqrt(square_sums / D + 1e-05)
    normed = (values * scale[:, :, None] * norm_gain[None, None, :]).astype(jnp.bfloat16)
    embedded = normed[None]
    grad_in = cotangent[0].astype(jnp.float32) * norm_gain[None, None, :]
    inner_sums = lax.psum(jnp.sum(grad_in * values, axis=2), ("group", "section", "tensor"))
    inner = inner_sums / D
    slot_grad = (scale[:, :, None] * grad_in - values * (scale**3 * inner)[:, :, None]).astype(
        jnp.bfloat16
    )
    returned = lax.all_to_all(slot_grad, "dp", split_axis=0, concat_axis=0, tiled=True)
    returned = returned.reshape(replicas * slots, columns)
    gathered = lax.dot_general(
        placer, returned, (((0,), (0,)), ((), ())), preferred_element_type=jnp.float32
    )
    back = (gathered * valid[:, None]).astype(jnp.bfloat16)
    input_terms = lax.dot_general(
        back, w_merge, (((1,), (1,)), ((), ())), preferred_element_type=jnp.float32
    )
    grad_merged = lax.psum_scatter(
        input_terms, ("group", "section", "tensor"), scatter_dimension=1, tiled=True
    )
    column_block = lax.all_to_all(merged, "dp", split_axis=1, concat_axis=0, tiled=True)
    grad_weight = lax.dot_general(
        column_block,
        lax.all_gather(back, "dp", axis=0, tiled=True),
        (((0,), (0,)), ((), ())),
        preferred_element_type=jnp.float32,
    )
    return (embedded, grad_merged, grad_weight)


def solution(mesh):
    placed = (
        P("dp", None),
        P("dp"),
        P("dp", None),
        P(None, ("group", "section", "tensor")),
        P(("group", "section", "tensor")),
        P("dp", None, None, ("group", "section", "tensor")),
    )
    return jax.shard_map(
        on_device,
        mesh=mesh,
        in_specs=placed,
        out_specs=(
            P("dp", None, None, ("group", "section", "tensor")),
            P("dp", ("group", "section", "tensor")),
            P("dp", ("group", "section", "tensor")),
        ),
        check_vma=False,
    )
```

profile of v0, /device:TPU:0, one launch (start us, length us, event | category | flops | bytes accessed | tf_op | source)
XLA Modules:
  0.0 182.4 jit_solution(6930971145670902794)
XLA Ops:
  8.0 0.0 all-gather.2.cloned.1.call-start
  8.1 0.7 iota_compare_fusion.3
  8.7 0.7 fusion.18
  9.5 1.2 reduce-window.6
  10.8 0.1 slice.12
  10.8 0.1 copy.23
  11.0 0.1 copy.24
  11.1 0.1 add_bitcast_fusion
  11.2 0.7 fusion.16
  11.9 0.7 multiply_add_fusion
  12.5 0.0 copy-start.2
  12.5 7.0 %convolution_convert_fusion = bf16[384,1024]{1,0:T(8,128)(2,1)S(1)} fusion(bf16[192,5120]{1,0:T(8,128)(2,1)} %param.6, bf16[5120,1024]{1,0:T(8,128)(2,1)} %param.9, f32[192]{0:T(256)S(1)} %compare_convert_fusion, s32[192]{0:T(256)S(1)} %multiply_add_fusion), kind=kOutput, calls=%fused_computation.14 | convolution fusion | flops 2165514240 | bytes 13239808 | tf_op jit(solution)/shard_map/dot_general | solution.py:31
  19.6 0.0 copy-start
  19.6 26.4 %all_to_all.29 = bf16[4,96,1024]{2,1,0:T(8,128)(2,1)S(1)} all-to-all(bf16[4,96,1024]{2,1,0:T(8,128)(2,1)S(1)} %bitcast.38), channel_id=1, replica_groups=mesh['group'=2,'dp'=4,'section'=2,'tensor'=2] {'dp'}, dimensions={0} | all-to-all | bytes 1572864 | tf_op jit(solution)/shard_map/all_to_all | solution.py:33
  46.0 0.0 copy-done.2
  46.0 0.0 copy-done
  46.0 0.4 fusion.3
  46.4 14.3 %all-reduce.1 = (f32[4,96]{1,0:T(4,128)S(1)}, f32[4,96]{1,0:T(4,128)S(1)}) all-reduce(f32[4,96]{1,0:T(4,128)S(1)} %get-tuple-element.19, f32[4,96]{1,0:T(4,128)S(1)} %get-tuple-element.18), channel_id=1, replica_groups=mesh['group'=2,'dp'=4,'section'=2,'tensor'=2] {'group','section','tensor'}, use_global_device_ids=true, to_apply=%region_5.6 | all-reduce | flops 768 | bytes 6144 | tf_op jit(solution)/shard_map/psum | solution.py:35
  60.7 1.4 fusion.5
  62.1 23.6 %all_to_all.30 = bf16[4,96,1024]{2,1,0:T(8,128)(2,1)S(1)} all-to-all(bf16[4,96,1024]{2,1,0:T(8,128)(2,1)S(1)} %get-tuple-element.22), channel_id=1, replica_groups=mesh['group'=2,'dp'=4,'section'=2,'tensor'=2] {'dp'}, dimensions={0} | all-to-all | bytes 1572864 | tf_op jit(solution)/shard_map/all_to_all | solution.py:45
  85.7 1.2 fusion.7
  86.9 0.0 all-gather.2.cloned.1.call-update
  86.9 0.0 reduce-scatter.2.cloned.1.call-start
  86.9 9.7 %fusion.21 = f32[192,5120]{1,0:T(8,128)} fusion(bf16[192,1024]{1,0:T(8,128)(2,1)} %fusion.7, bf16[5120,1024]{1,0:T(8,128)(2,1)} %param.9), kind=kOutput, calls=%fused_computation.48 | convolution fusion | flops 2013265920 | bytes 14811136 | tf_op jit(solution)/shard_map/dot_general | solution.py:51
  96.7 0.0 reduce-scatter.2.cloned.1.call-update
  96.7 1.5 copy-done.1
  98.2 0.1 copy.31
  98.3 64.7 %all_to_all.31 = bf16[192,4,1280]{2,0,1:T(8,128)(2,1)S(1)} all-to-all(bf16[192,4,1280]{2,0,1:T(8,128)(2,1)S(1)} %bitcast.34), channel_id=1, replica_groups=mesh['group'=2,'dp'=4,'section'=2,'tensor'=2] {'dp'}, dimensions={1} | all-to-all | bytes 3932160 | tf_op jit(solution)/shard_map/all_to_all | solution.py:57
  163.1 0.0 all-gather.2.cloned.1.call-done
  163.1 6.0 %convolution_bitcast_fusion = f32[1280,1024]{0,1:T(8,128)} fusion(bf16[768,1024]{1,0:T(8,128)(2,1)} %all-gather.2.cloned.1.call-done, bf16[768,1280]{1,0:T(8,128)(2,1)S(1)} %bitcast.37), kind=kOutput, calls=%fused_computation | convolution fusion | flops 2013265920 | bytes 8781824 | tf_op jit(solution)/shard_map/dot_general | solution.py:58
  169.1 5.9 %copy.26 = f32[1280,1024]{1,0:T(8,128)} copy(f32[1280,1024]{0,1:T(8,128)} %convolution_bitcast_fusion) | data formatting | bytes 10485760
  174.9 0.0 reduce-scatter.2.cloned.1.call-done
  (9 shorter events, 0.1 us)
Async XLA Ops:
  8.0 155.1 %all-gather.2.cloned.1.call-start = ((), (), s32[]{:S(2)}) async-start(), calls=%async_computation.5 | async-start | bytes 1966080 | tf_op jit(solution)/shard_map/all_gather | solution.py:60
  12.5 33.4 %copy-start.2 = (f32[1024]{0:T(1024)S(1)}, f32[1024]{0:T(1024)}, u32[]{:S(2)}) copy-start(f32[1024]{0:T(1024)} %param.10) | copy-start | bytes 12292
  19.6 26.4 %copy-start = (bf16[1,4,96,1024]{3,2,1,0:T(8,128)(2,1)S(1)}, bf16[1,4,96,1024]{3,2,1,0:T(8,128)(2,1)}, u32[]{:S(2)}) copy-start(bf16[1,4,96,1024]{3,2,1,0:T(8,128)(2,1)} %param.11) | copy-start | bytes 2359300
  86.9 88.1 %reduce-scatter.2.cloned.1.call-start = ((), (), s32[]{:S(2)}) async-start(), calls=%async_computation.4 | async-start | bytes 4423680 | tf_op jit(solution)/shard_map/reduce_scatter | solution.py:54
  96.7 1.5 copy-start.1
Sparse Core Ops, SparseCore 0:
  87.0 58.4 all-gather.1
Sparse Core Ops, SparseCore 1:
  96.8 46.7 reduce-scatter.1
where the time goes:
time: 183 us; the launch traced here: 182 us
  blocking collectives  129 us (70%)
  matrix products  23.9 us (13%)
  between operations  15.5 us (8%)
  local copies, waits for them, and re-layouts  7.84 us (4%)
  other arithmetic  6.04 us (3%)
    all_to_all x1, blocking collectives, on_device(): lax.all_to_all(merged, 'dp', split_axis=1, concat_axis=0, tiled=True)  64.7 us
    all_to_all x1, blocking collectives, on_device(): lax.all_to_all(outgoing, 'dp', split_axis=0, concat_axis=0, tiled=True)  26.4 us
    all_to_all x1, blocking collectives, on_device(): lax.all_to_all(slot_grad, 'dp', split_axis=0, concat_axis=0, tiled=True)  23.6 us
    psum x1, blocking collectives, on_device(): lax.psum(jnp.sum(values * values, axis=2), ('group', 'section', 'tensor'))  14.3 us
    dot_general x1, matrix products, on_device(): lax.dot_general(back, w_merge, (((1,), (1,)), ((), ())), preferred_elemen...  9.72 us
    unnamed x8, local copies, waits for them, and re-layouts  7.42 us
    dot_general x1, matrix products, on_device(): jnp.dot(placer, masked, preferred_element_type=jnp.float32)  7.02 us
    dot_general x1, matrix products, on_device(): lax.dot_general(column_block, lax.all_gather(back, 'dp', axis=0, tiled=Tr...  5.97 us
  transfers between devices with their start and end apart: 2, of which 0 were waited for; matrix products, arithmetic and copies ran while one was open for 12% of the time, Pallas kernels for 0%

commit v1 on v0

--- a/solution.py
+++ b/solution.py
@@ -32,7 +32,9 @@
     outgoing = outgoing.reshape(replicas, slots, columns)
     received = lax.all_to_all(outgoing, "dp", split_axis=0, concat_axis=0, tiled=True)
     values = received.astype(jnp.float32)
-    square_sums = lax.psum(jnp.sum(values * values, axis=2), ("group", "section", "tensor"))
+    square_sums = jnp.sum(
+        lax.all_gather(jnp.sum(values * values, axis=2), ("group", "section", "tensor")), axis=0
+    )
     scale = lax.rsqrt(square_sums / D + 1e-05)
     normed = (values * scale[:, :, None] * norm_gain[None, None, :]).astype(jnp.bfloat16)
     embedded = normed[None]

time: 183 us -> 203 us (1.11)
  blocking collectives: 129 us -> 149 us
    all_gather x0 -> x1, blocking collectives: none -> 19.9 us  [on_device(): lax.all_gather(jnp.sum(values * values, axis=2), ('group', 'section', 'te...]
  transfers between devices with their start and end apart: 2 -> 2, of which waited for: 0 -> 0; matrix products, arithmetic and copies ran while one was open for 12% -> 11% of each run, Pallas kernels for 0% -> 0%
where the time goes in v1:
time: 203 us
  blocking collectives  149 us (73%)
  matrix products  23.9 us (12%)
  between operations  15.5 us (8%)
  local copies, waits for them, and re-layouts  7.84 us (4%)
  other arithmetic  6.06 us (3%)
    all_to_all x1, blocking collectives, on_device(): lax.all_to_all(merged, 'dp', split_axis=1, concat_axis=0, tiled=True)  64.7 us
    all_to_all x1, blocking collectives, on_device(): lax.all_to_all(outgoing, 'dp', split_axis=0, concat_axis=0, tiled=True)  26.4 us
    all_to_all x1, blocking collectives, on_device(): lax.all_to_all(slot_grad, 'dp', split_axis=0, concat_axis=0, tiled=True)  24 us
    all_gather x1, blocking collectives, on_device(): lax.all_gather(jnp.sum(values * values, axis=2), ('group', 'section', 'te...  19.9 us
    psum x1, blocking collectives, on_device(): lax.psum(jnp.sum(grad_in * values, axis=2), ('group', 'section', 'tensor'))  14.3 us
    dot_general x1, matrix products, on_device(): lax.dot_general(back, w_merge, (((1,), (1,)), ((), ())), preferred_elemen...  9.73 us
    unnamed x8, local copies, waits for them, and re-layouts  7.42 us
    dot_general x1, matrix products, on_device(): jnp.dot(placer, masked, preferred_element_type=jnp.float32)  7.02 us
  transfers between devices with their start and end apart: 2, of which 0 were waited for; matrix products, arithmetic and copies ran while one was open for 11% of the time, Pallas kernels for 0%

profile of v1, /device:TPU:0, one launch (start us, length us, event | category | flops | bytes accessed | tf_op | source)
XLA Modules:
  0.0 202.6 jit_solution(12734765205774224603)
XLA Ops:
  8.0 0.0 all-gather.4.cloned.1.call-start
  8.1 0.7 iota_compare_fusion.3
  8.7 0.7 fusion.18
  9.5 1.2 reduce-window.6
  10.8 0.1 slice.12
  10.8 0.1 copy.23
  11.0 0.1 copy.24
  11.1 0.1 add_bitcast_fusion
  11.2 0.7 fusion.16
  11.9 0.7 multiply_add_fusion
  12.5 0.0 copy-start.2
  12.5 7.0 %convolution_convert_fusion = bf16[384,1024]{1,0:T(8,128)(2,1)S(1)} fusion(bf16[192,5120]{1,0:T(8,128)(2,1)} %param.6, bf16[5120,1024]{1,0:T(8,128)(2,1)} %param.9, f32[192]{0:T(256)S(1)} %compare_convert_fusion, s32[192]{0:T(256)S(1)} %multiply_add_fusion), kind=kOutput, calls=%fused_computation.14 | convolution fusion | flops 2165514240 | bytes 13239808 | tf_op jit(solution)/shard_map/dot_general | solution.py:31
  19.6 0.0 copy-start
  19.6 26.4 %all_to_all.29 = bf16[4,96,1024]{2,1,0:T(8,128)(2,1)S(1)} all-to-all(bf16[4,96,1024]{2,1,0:T(8,128)(2,1)S(1)} %bitcast.39), channel_id=1, replica_groups=mesh['group'=2,'dp'=4,'section'=2,'tensor'=2] {'dp'}, dimensions={0} | all-to-all | bytes 1572864 | tf_op jit(solution)/shard_map/all_to_all | solution.py:33
  46.0 0.0 copy-done.2
  46.0 0.0 copy-done
  46.0 0.4 fusion.3
  46.4 14.3 %psum.7 = f32[4,96]{1,0:T(4,128)S(1)} all-reduce(f32[4,96]{1,0:T(4,128)S(1)} %get-tuple-element.18), channel_id=1, replica_groups=mesh['group'=2,'dp'=4,'section'=2,'tensor'=2] {'group','section','tensor'}, use_global_device_ids=true, to_apply=%region_7.8 | all-reduce | flops 384 | bytes 3072 | tf_op jit(solution)/shard_map/psum | solution.py:42
  60.7 19.9 %all-gather.1 = f32[8,4,96]{2,1,0:T(4,128)S(1)} all-gather(f32[1,4,96]{2,1,0:T(4,128)S(1)} %bitcast.44), channel_id=2, replica_groups=mesh['group'=2,'dp'=4,'section'=2,'tensor'=2] {'group','section','tensor'}, dimensions={0}, use_global_device_ids=true | all-gather | bytes 13824 | tf_op jit(solution)/shard_map/all_gather | solution.py:36
  80.6 1.4 fusion.5
  82.0 24.0 %all_to_all.30 = bf16[4,96,1024]{2,1,0:T(8,128)(2,1)S(1)} all-to-all(bf16[4,96,1024]{2,1,0:T(8,128)(2,1)S(1)} %get-tuple-element.20), channel_id=1, replica_groups=mesh['group'=2,'dp'=4,'section'=2,'tensor'=2] {'dp'}, dimensions={0} | all-to-all | bytes 1572864 | tf_op jit(solution)/shard_map/all_to_all | solution.py:47
  105.9 1.2 fusion.7
  107.1 0.0 all-gather.4.cloned.1.call-update
  107.1 0.0 reduce-scatter.2.cloned.1.call-start
  107.2 9.7 %fusion.21 = f32[192,5120]{1,0:T(8,128)} fusion(bf16[192,1024]{1,0:T(8,128)(2,1)} %fusion.7, bf16[5120,1024]{1,0:T(8,128)(2,1)} %param.9), kind=kOutput, calls=%fused_computation.48 | convolution fusion | flops 2013265920 | bytes 14811136 | tf_op jit(solution)/shard_map/dot_general | solution.py:53
  116.9 0.0 copy-start.1
  116.9 0.0 reduce-scatter.2.cloned.1.call-update
  116.9 1.5 copy-done.1
  118.5 0.1 copy.31
  118.6 64.7 %all_to_all.31 = bf16[192,4,1280]{2,0,1:T(8,128)(2,1)S(1)} all-to-all(bf16[192,4,1280]{2,0,1:T(8,128)(2,1)S(1)} %bitcast.35), channel_id=1, replica_groups=mesh['group'=2,'dp'=4,'section'=2,'tensor'=2] {'dp'}, dimensions={1} | all-to-all | bytes 3932160 | tf_op jit(solution)/shard_map/all_to_all | solution.py:59
  183.3 6.0 %convolution_bitcast_fusion = f32[1280,1024]{0,1:T(8,128)} fusion(bf16[768,1024]{1,0:T(8,128)(2,1)} %all-gather.4.cloned.1.call-done, bf16[768,1280]{1,0:T(8,128)(2,1)S(1)} %bitcast.38), kind=kOutput, calls=%fused_computation | convolution fusion | flops 2013265920 | bytes 8781824 | tf_op jit(solution)/shard_map/dot_general | solution.py:60
  189.2 5.9 %copy.26 = f32[1280,1024]{1,0:T(8,128)} copy(f32[1280,1024]{0,1:T(8,128)} %convolution_bitcast_fusion) | data formatting | bytes 10485760
  (11 shorter events, 0.1 us)
Async XLA Ops:
  8.0 175.3 %all-gather.4.cloned.1.call-start = ((), (), s32[]{:S(2)}) async-start(), calls=%async_computation.5 | async-start | bytes 1966080 | tf_op jit(solution)/shard_map/all_gather | solution.py:62
  12.5 33.4 %copy-start.2 = (f32[1024]{0:T(1024)S(1)}, f32[1024]{0:T(1024)}, u32[]{:S(2)}) copy-start(f32[1024]{0:T(1024)} %param.10) | copy-start | bytes 12292
  19.6 26.4 %copy-start = (bf16[1,4,96,1024]{3,2,1,0:T(8,128)(2,1)S(1)}, bf16[1,4,96,1024]{3,2,1,0:T(8,128)(2,1)}, u32[]{:S(2)}) copy-start(bf16[1,4,96,1024]{3,2,1,0:T(8,128)(2,1)} %param.11) | copy-start | bytes 2359300
  107.1 88.0 %reduce-scatter.2.cloned.1.call-start = ((), (), s32[]{:S(2)}) async-start(), calls=%async_computation.4 | async-start | bytes 4423680 | tf_op jit(solution)/shard_map/reduce_scatter | solution.py:56
  116.9 1.6 copy-start.1
Sparse Core Ops, SparseCore 0:
  107.3 57.0 all-gather.3
Sparse Core Ops, SparseCore 1:
  117.0 46.6 reduce-scatter.1
